TPU v7x, 512 devices: a whole 4x8x8 slice. The times are simulated.
512 devices in a mesh: lat: 128 (over z, y, core), tok: 4 (over x).
Axes of the slice: x: 4, y: 8, z: 8, core: 2. Of those that a mesh axis runs over, the one named last changes fastest.
Arguments:
- resid_stream: bfloat16 [384, 8192], P('lat', 'tok'), may hold values from -6 to 6
- enc_weight: bfloat16 [16384, 8192], P('lat', 'tok'), may hold values from -0.0625 to 0.0625
- enc_bias: float32 [16384], P('lat'), may hold values from -3 to 3
- dec_weight: bfloat16 [16384, 8192], P('lat', 'tok'), may hold values from -0.75 to 0.75
- dec_bias: float32 [8192], P('tok'), may hold values from -3 to 3
- active_ids: int32 [384, 64], replicated, may hold values from 0 to 16383, as said below
- active_count: int32 [384], replicated, may hold values from 32 to 64, as said below
Outputs:
- pre_acts: float32 [384, 16384], P(None, 'lat')
- residual: bfloat16 [384, 8192], P('lat', 'tok')
- grad_enc: bfloat16 [16384, 8192], P('lat', 'tok')
- grad_dec: bfloat16 [16384, 8192], P('lat', 'tok')
Inputs may be any that keep to these rules, and one draw needn't show every extreme that they name: `active_ids`: within a row all 64 entries are different latents; entries past the row's count are ordinary latent numbers that are to be ignored; some latent shards are named far more often than others. `active_count`: some row has 64 valid entries and some has 32.
All inputs are finite; a program needn't handle non-finite values.
Results may differ from a plain program's by a relative error of at most 0.0059.
Values may be sent and summed in bfloat16 or wider, within the bound.
A program may use at most 64 MiB of HBM per device.

v0:
```python
import math

import jax
import jax.numpy as jnp
from jax import lax
from jax.sharding import PartitionSpec as P


def active_mask(id_rows, counts, first_latent, latent_count):
    tokens, top_count = id_rows.shape
    block_rows = math.gcd(tokens, 128)
    in_list = jnp.arange(top_count, dtype=jnp.int32)[None, :] < counts[:, None]
    local_ids = jnp.where(in_list, id_rows - first_latent, -1)
    latent_iota = jnp.arange(latent_count, dtype=jnp.int32)

    def one_block(id_block):
        return jnp.any(id_block[:, :, None] == latent_iota[None, None, :], axis=1).astype(
            jnp.float32
        )

    blocks = lax.map(one_block, local_ids.reshape(tokens // block_rows, block_rows, top_count))
    return blocks.reshape(tokens, latent_count)


def shards(resid_stream, enc_weight, enc_bias, dec_weight, dec_bias, active_ids, active_count):
    lat_dev = enc_weight.shape[0]
    rows_own = resid_stream.shape[0]
    full_rows = lax.all_gather(resid_stream, "lat", axis=0, tiled=True)
    partial_value = lax.dot_general(
        full_rows, enc_weight, (((1,), (1,)), ((), ())), preferred_element_type=jnp.float32
    )
    pre_acts = lax.psum(partial_value, "tok") + enc_bias[None, :]
    act_mask = active_mask(active_ids, active_count, lax.axis_index("lat") * lat_dev, lat_dev)
    activations = (pre_acts * act_mask).astype(jnp.bfloat16)
    own_start = lax.axis_index("lat") * rows_own
    rebuilt = lax.psum(jnp.dot(activations, dec_weight, preferred_element_type=jnp.float32), "lat")
    residual_all = (rebuilt + dec_bias[None, :] - full_rows.astype(jnp.float32)).astype(
        jnp.bfloat16
    )
    residual = lax.dynamic_slice_in_dim(residual_all, own_start, rows_own, 0)
    grad_dec = 0.5 * lax.dot_general(
        activations, residual_all, (((0,), (0,)), ((), ())), preferred_element_type=jnp.float32
    )
    back_terms = lax.dot_general(
        residual_all, dec_weight, (((1,), (1,)), ((), ())), preferred_element_type=jnp.float32
    )
    back_terms = lax.psum(back_terms, "tok")
    act_grads = (0.5 * back_terms * act_mask).astype(jnp.bfloat16)
    grad_enc = lax.dot_general(
        act_grads, full_rows, (((0,), (0,)), ((), ())), preferred_element_type=jnp.float32
    )
    return (pre_acts, residual, grad_enc.astype(jnp.bfloat16), grad_dec.astype(jnp.bfloat16))


def solution(mesh):
    placed = (P("lat", "tok"), P("lat", "tok"), P("lat"), P("lat", "tok"), P("tok"), P(), P())
    return jax.shard_map(
        shards,
        mesh=mesh,
        in_specs=placed,
        out_specs=(P(None, "lat"), P("lat", "tok"), P("lat", "tok"), P("lat", "tok")),
        check_vma=False,
    )
```

profile of v0, /device:TPU:1, one launch (start us, length us, event | category | flops | bytes accessed | tf_op | source)
XLA Modules:
  0.0 426.8 jit_solution(15382301777076680504)
XLA Ops:
  7.2 0.0 copy-start
  7.2 0.0 all-gather.3.cloned.1.call-start
  7.2 0.7 all-gather.3.cloned.1.call-update
  7.9 0.0 all-reduce.4.cloned.1.call-start
  8.0 0.9 subtract_select_fusion
  8.9 0.1 copy.14
  9.0 0.0 copy-start.2
  9.0 91.1 %all-gather.3.cloned.1.call-done = bf16[128,3,2048]{2,1,0:T(4,128)(2,1)} async-done(((bf16[1,3,2048]{2,1,0:T(4,128)(2,1)}), bf16[128,3,2048]{2,1,0:T(4,128)(2,1)}) %all-gather.3.cloned.1.call-update) | async-done | bytes 1572880 | tf_op jit(solution)/shard_map/all_gather | solution.py:28
  100.1 3.9 reshape.33
  104.0 0.0 copy-done.2
  104.0 0.0 copy-start.4
  104.0 1.3 fusion.6
  105.3 0.0 all-reduce.4.cloned.1.call-update
  105.3 0.0 all-reduce.6.cloned.1.call-start
  105.4 4.4 %while.11 = (s32[]{:T(128)}, f32[3,128,128]{2,1,0:T(8,128)S(1)}, s32[3,128,64]{2,1,0:T(8,128)S(1)}, s32[]{:T(128)}) while((s32[]{:T(128)}, f32[3,128,128]{2,1,0:T(8,128)S(1)}, s32[3,128,64]{2,1,0:T(8,128)S(1)}, s32[]{:T(128)}) %tuple.37), condition=%wide.region_3.4_spmd.clone, body=%wide.region_1.3_spmd.clone.sunk | while | flops 2097154 | bytes 196677 | solution.py:21
  105.4 1.4 fusion.20
  106.9 1.4 fusion.20
  108.3 1.4 fusion.20
  109.8 42.4 %all-reduce.4.cloned.1.call-done = f32[384,128]{1,0:T(8,128)} async-done(((f32[384,128]{1,0:T(8,128)}), f32[384,128]{1,0:T(8,128)}) %all-reduce.4.cloned.1.call-update) | async-done | bytes 196624 | tf_op jit(solution)/shard_map/psum | solution.py:32
  152.2 0.0 copy-done.4
  152.2 1.6 fusion.4
  153.8 0.0 copy-done
  153.8 2.2 fusion.7
  156.1 0.0 copy-start.3
  156.1 0.0 all-reduce.6.cloned.1.call-update
  156.1 0.0 all-reduce.8.cloned.1.call-start
  156.1 206.2 %all-reduce.6.cloned.1.call-done = f32[384,2048]{1,0:T(8,128)} async-done(((f32[384,2048]{1,0:T(8,128)}), f32[384,2048]{1,0:T(8,128)}) %all-reduce.6.cloned.1.call-update) | async-done | bytes 3145744 | tf_op jit(solution)/shard_map/psum | solution.py:36
  362.3 0.0 copy-done.3
  362.3 2.4 subtract_convert_fusion
  364.8 0.0 copy-start.1
  364.8 1.1 copy-done.1
  365.9 1.3 fusion.8
  367.2 2.7 fusion.3
  369.9 0.0 all-reduce.8.cloned.1.call-update
  369.9 1.5 constant_dynamic-slice_fusion
  371.4 46.7 %all-reduce.8.cloned.1.call-done = f32[384,128]{1,0:T(8,128)} async-done(((f32[384,128]{1,0:T(8,128)}), f32[384,128]{1,0:T(8,128)}) %all-reduce.8.cloned.1.call-update) | async-done | bytes 196624 | tf_op jit(solution)/shard_map/psum | solution.py:47
  418.1 1.0 fusion.5
  419.0 1.3 convolution_convert_fusion
  (7 shorter events, 0.1 us)
Async XLA Ops:
  7.2 146.7 %copy-start = (bf16[128,2048]{1,0:T(8,128)(2,1)S(1)}, bf16[128,2048]{1,0:T(8,128)(2,1)}, u32[]{:S(2)}) copy-start(bf16[128,2048]{1,0:T(8,128)(2,1)} %param.12) | copy-start | bytes 1572868
  7.2 92.9 %all-gather.3.cloned.1.call-start = ((), (), s32[]{:S(2)}) async-start(), calls=%async_computation.3 | async-start | bytes 2113536 | tf_op jit(solution)/shard_map/all_gather | solution.py:28
  7.9 144.3 %all-reduce.4.cloned.1.call-start = ((), (), s32[]{:S(2)}) async-start(), calls=%async_computation | async-start | bytes 393216 | tf_op jit(solution)/shard_map/psum | solution.py:32
  9.0 95.0 %copy-start.2 = (bf16[128,2048]{1,0:T(8,128)(2,1)S(1)}, bf16[128,2048]{1,0:T(8,128)(2,1)}, u32[]{:S(2)}) copy-start(bf16[128,2048]{1,0:T(8,128)(2,1)} %param.10) | copy-start | bytes 1572868
  104.0 48.1 %copy-start.4 = (f32[128]{0:T(128)S(1)}, f32[128]{0:T(128)}, u32[]{:S(2)}) copy-start(f32[128]{0:T(128)} %param.11) | copy-start | bytes 1540
  105.3 257.0 %all-reduce.6.cloned.1.call-start = ((), (), s32[]{:S(2)}) async-start(), calls=%async_computation.1 | async-start | bytes 6291456 | tf_op jit(solution)/shard_map/psum | solution.py:36
  156.1 206.3 %copy-start.3 = (f32[2048]{0:T(1024)S(1)}, f32[2048]{0:T(1024)}, u32[]{:S(2)}) copy-start(f32[2048]{0:T(1024)} %param.13) | copy-start | bytes 24580
  156.1 262.0 %all-reduce.8.cloned.1.call-start = ((), (), s32[]{:S(2)}) async-start(), calls=%async_computation.2 | async-start | bytes 393216 | tf_op jit(solution)/shard_map/psum | solution.py:47
  364.8 1.1 copy-start.1
Sparse Core Ops, SparseCore 0:
  11.1 88.9 all-gather.2
  105.4 46.6 all-reduce.3
  156.2 206.0 all-reduce.5
  370.0 47.9 all-reduce.7
where the time goes:
time: 428 us; the launch traced here: 427 us
  waiting for transfers between devices  387 us (90%)
  between operations  13.9 us (3%)
  other arithmetic  10.2 us (2%)
  matrix products  8.73 us (2%)
  local copies, waits for them, and re-layouts  6.7 us (2%)
    psum x1, waiting for transfers between devices, shards(): lax.psum(jnp.dot(activations, dec_weight, preferred_element_type=jnp.floa...  206 us
    all_gather x1, waiting for transfers between devices, shards(): full_rows = lax.all_gather(resid_stream, 'lat', axis=0, tiled=True)  91.1 us
    psum x1, waiting for transfers between devices, shards(): back_terms = lax.psum(back_terms, 'tok')  46.7 us
    psum x1, waiting for transfers between devices, shards(): pre_acts = lax.psum(partial_value, 'tok') + enc_bias[None, :]  42.4 us
  transfers between devices with their start and end apart: 4, of which 4 were waited for; matrix products, arithmetic and copies ran while one was open for 2% of the time, Pallas kernels for 0%

commit v1 on v0

v1 whole, which is shorter than its diff:
```python
import functools
import math

import jax
import jax.numpy as jnp
from jax import lax
from jax.experimental import pallas as pl
from jax.experimental.pallas import tpu as pltpu
from jax.sharding import PartitionSpec as P

F32 = jnp.float32
BF16 = jnp.bfloat16
MESH = pl.DeviceIdType.MESH


def divisor(limit, by):
    s = 16
    m = (1 << s) // by + 1
    assert all((i * m) >> s == i // by for i in range(limit))
    return m, s


class Dims:
    def __init__(self, mesh, rows_own, width, lat_dev, top_count):
        self.X = mesh.shape["tok"]
        self.n = math.isqrt(mesh.shape["lat"] // 2)
        assert self.n * self.n * 2 == mesh.shape["lat"]
        self.own = rows_own
        self.rows = rows_own * mesh.shape["lat"]
        self.block = self.rows // self.n
        self.width = width // 2
        self.lanes = self.width // 128
        self.flat = rows_own * self.lanes
        self.lat = lat_dev
        self.top = top_count
        self.chunk = self.rows // self.X


def kernel(
    dm,
    x_ref, ids_ref, cnt_ref, eb_ref, db_ref, enc_ref, dec_ref,
    pre_out, res_out, ge_out, gd_out,
    F, R1, Xraw, XF, WE, WD, PS, PR, SUM, RX, mask, act_s, act_f, pre_s, pre_f,
    T, RB, Q, RQ, RES, RESF, ag_s, ag_f,
    send, recv, local,
):
    n, X, own, block, width, lanes, flat = dm.n, dm.X, dm.own, dm.block, dm.width, dm.lanes, dm.flat
    rows, lat, chunk, half = dm.rows, dm.lat, dm.chunk, dm.width // 2
    depth = n // 2
    L = lax.axis_index("lat")
    t = lax.axis_index("tok")
    c = lax.rem(L, 2)
    chip = L // 2
    y = lax.rem(chip, n)
    z = chip // n
    a = y + c * (z - y)
    b = z + c * (y - z)
    partner = L + 1 - 2 * c

    def lat_of(ap, bp):
        yy = ap + c * (bp - ap)
        zz = bp + c * (ap - bp)
        return (zz * n + yy) * 2 + c

    count = {"copy": 0, "local": 0}
    sends = []

    def wrap(v, m):
        return lax.rem(v + 2 * m, m)

    def remote(src, dst, lat_id, tok_id, recv_index=None):
        k = count["copy"]
        count["copy"] += 1
        r = k if recv_index is None else recv_index
        d = pltpu.make_async_remote_copy(
            src_ref=src, dst_ref=dst, send_sem=send.at[k], recv_sem=recv.at[r],
            device_id=(lat_id, tok_id), device_id_type=MESH,
        )
        return d

    def go(d):
        d.start()
        sends.append(d)
        return d

    def copy_local(src, dst):
        k = count["local"]
        count["local"] += 1
        d = pltpu.make_async_copy(src, dst, local.at[k])
        d.start()
        return d

    barrier = pltpu.get_barrier_semaphore()
    heard = 0

    def greet(lat_id, tok_id):
        pl.semaphore_signal(barrier, inc=1, device_id=(lat_id, tok_id), device_id_type=MESH)

    greet(partner, t)
    heard += 1
    for d in range(1, n):
        for other in (0, 1):
            dev = lat_of(wrap(a + d, n), b)
            greet(dev + other * (1 - 2 * c), t)
    heard += 2 * (n - 1)
    for s in (1, -1):
        greet(lat_of(a, wrap(b + s, n)), t)
    heard += 2
    for d in range(1, X):
        for dev in (L, partner):
            greet(dev, wrap(t + d, X))
    heard += 2 * (X - 1)

    xv = x_ref[...].astype(F32)
    for r in range(own):
        for j in range(2 * lanes):
            F[j // lanes, r * lanes + j % lanes : r * lanes + j % lanes + 1, :] = xv[
                r : r + 1, j * 128 : (j + 1) * 128
            ]

    pl.semaphore_wait(barrier, heard)

    recv1 = count["copy"]
    count["copy"] += 2 * n

    def slot1(pos, core):
        return pl.ds(pl.multiple_of((pos * 2 + core) * flat, 8), flat)

    go(remote(F.at[1 - c], R1.at[slot1(y + (1 - c) * (z - y), c)], partner, t, recv1 + c))
    for d in range(1, n):
        for h in (0, 1):
            pos = (y, z)[h]
            yy = wrap(y + d, n) if h == 0 else y
            zz = wrap(z + d, n) if h == 1 else z
            go(remote(F.at[h], R1.at[slot1(pos, c)], (zz * n + yy) * 2 + h, t, recv1 + 2 * d + c))
    mine = F[c]
    R1[slot1(a, c), :] = mine

    own_cols = pl.ds(pl.multiple_of(c * width, 128), width)
    far_cols = pl.ds(pl.multiple_of((1 - c) * width, 128), width)
    own_lats = pl.ds(pl.multiple_of(c * lat, lat), lat)
    w_local = [copy_local(enc_ref.at[:, own_cols], WE.at[own_lats]), copy_local(dec_ref.at[:, own_cols], WD.at[own_lats])]
    w_remote = [
        go(remote(enc_ref.at[:, far_cols], WE.at[own_lats], partner, t)),
        go(remote(dec_ref.at[:, far_cols], WD.at[own_lats], partner, t)),
    ]

    my_rows = pl.ds(pl.multiple_of(t * chunk, 8), chunk)
    cnt_row = cnt_ref[...].astype(F32)
    row_i = lax.broadcasted_iota(jnp.int32, (chunk, rows), 0) + t * chunk
    col_i = lax.broadcasted_iota(jnp.int32, (chunk, rows), 1)
    cnt_col = jnp.sum(
        jnp.where(row_i == col_i, jnp.broadcast_to(cnt_row, (chunk, rows)), 0.0), axis=1, keepdims=True
    )
    k_i = lax.broadcasted_iota(jnp.int32, (chunk, dm.top), 1).astype(F32)
    local_ids = jnp.where(k_i < cnt_col, ids_ref[my_rows, :] - L * lat, -1)
    lane_i = lax.broadcasted_iota(jnp.int32, (chunk, lat), 1)
    m = jnp.zeros((chunk, lat), F32)
    for k in range(dm.top):
        m = jnp.where(local_ids[:, k : k + 1] == lane_i, 1.0, m)
    mask[...] = m

    m1, s1 = divisor(rows, block)
    m2, s2 = divisor(block, block // n)
    i0 = lax.broadcasted_iota(jnp.int32, (rows, rows), 0)
    i1 = lax.broadcasted_iota(jnp.int32, (rows, rows), 1)
    hi = (i0 * m1) >> s1
    rest = i0 - hi * block
    mid = (rest * m2) >> s2
    low = rest - mid * (block // n)
    order = i0 + c * (mid * block + hi * (block // n) + low - i0)
    perm = jnp.where(order == i1, 1.0, 0.0).astype(BF16)

    def remote_wait(index):
        pltpu.make_async_remote_copy(
            src_ref=F.at[0], dst_ref=R1.at[pl.ds(0, flat)], send_sem=send.at[0], recv_sem=recv.at[index],
            device_id=(partner, t), device_id_type=MESH,
        ).wait_recv()

    remote_wait(recv1 + 1 - c)
    for d in range(1, n):
        for core in (0, 1):
            remote_wait(recv1 + 2 * d + core)
    my_block = pl.ds(pl.multiple_of(b * block, 16), block)
    for j in range(lanes):
        Xraw[my_block, j * 128 : (j + 1) * 128] = R1[pl.ds(j, block, stride=lanes), :].astype(BF16)

    def ring_gather(buf):
        def piece(blk, h):
            return buf.at[pl.ds(pl.multiple_of(blk * block, 16), block), pl.ds(h * half, half)]

        flying = {}

        def send_step(way, s, h):
            blk = wrap(b - way * (s - 1), n)
            flying[way, s, h] = go(remote(piece(blk, h), piece(blk, h), lat_of(a, wrap(b + way, n)), t))

        for s in range(1, depth + 1):
            for o in (0, 1):
                for way in (1, -1):
                    first = 0 if way == 1 else 1
                    h = first if o == 0 else 1 - first
                    if s > 1:
                        flying[way, s - 1, h].wait_recv()
                    if s < depth or h == first:
                        send_step(way, s, h)
        flying[1, depth, 0].wait_recv()
        flying[-1, depth, 1].wait_recv()

    ring_gather(Xraw)

    for w in w_local:
        w.wait()
    for w in w_remote:
        w.wait_recv()

    xp = jnp.dot(perm, Xraw[...], preferred_element_type=F32).astype(BF16)
    XF[c] = xp
    x_swap = go(remote(XF.at[c], XF.at[c], partner, t))

    def feature_sum(u, part):
        PS[u, 0] = part[:, :lat]
        PS[u, 1] = part[:, lat:]
        d = go(remote(PS.at[u, 1 - c], PR.at[u], partner, t))
        d.wait_recv()
        SUM[u] = PS[u, c] + PR[u]
        arrive = []
        for d in range(1, X):
            to = wrap(t + d, X)
            arrive.append(go(remote(SUM.at[u, pl.ds(pl.multiple_of(to * chunk, 8), chunk)], RX.at[u, d - 1], L, to)))
        total = SUM[u, my_rows, :]
        for d in range(1, X):
            arrive[d - 1].wait_recv()
            total = total + RX[u, d - 1]
        return total

    nt = (((1,), (1,)), ((), ()))
    tn = (((0,), (0,)), ((), ()))
    part = lax.dot_general(XF[c], WE[...], nt, preferred_element_type=F32)
    pre = feature_sum(0, part) + eb_ref[...]
    act_s[...] = (pre * mask[...]).astype(BF16)
    pre_s[...] = pre
    act_rows = pl.ds(pl.multiple_of(t * chunk, 16), chunk)
    act_cols = pl.ds(pl.multiple_of(c * lat, lat), lat)
    act_recv = []
    for d in range(1, X):
        to = wrap(t + d, X)
        for swap in (0, 1):
            dev = L + swap * (1 - 2 * c)
            act_recv.append(go(remote(act_s, act_f.at[act_rows, act_cols], dev, to)))
    act_recv.append(go(remote(act_s, act_f.at[act_rows, act_cols], partner, t)))
    act_f[act_rows, act_cols] = act_s[...]
    pre_recv = []
    for d in range(1, X):
        pre_recv.append(go(remote(pre_s, pre_f.at[my_rows], L, wrap(t + d, X))))
    pre_f[my_rows, :] = pre
    for d in act_recv:
        d.wait_recv()

    T[...] = jnp.dot(act_f[...], WD[...], preferred_element_type=F32)

    flying = {}
    for s in range(1, depth + 1):
        for o in (0, 1):
            for way in (1, -1):
                first = 0 if way == 1 else 1
                h = first if o == 0 else 1 - first
                if s == 1 and h != first:
                    continue
                target = wrap(b + way * (depth + 1 - s), n)
                at = pl.ds(pl.multiple_of(target * block, 8), block)
                cols = pl.ds(h * half, half)
                w = 0 if way == 1 else 1
                if s > (1 if h == first else 2):
                    flying[way, s - 1, h].wait_recv()
                    T[at, cols] = T[at, cols] + RB[w, s - 2, :, cols]
                flying[way, s, h] = go(
                    remote(T.at[at, cols], RB.at[w, s - 1, :, cols], lat_of(a, wrap(b + way, n)), t)
                )
    q = T[my_block, :]
    for o in (0, 1):
        for way in (1, -1):
            flying[way, depth, (0 if way == 1 else 1) ^ o].wait_recv()
    q = q + RB[0, depth - 1] + RB[1, depth - 1]
    for j in range(n):
        Q[j] = q[:, j * 128 : (j + 1) * 128]
    q_recv = []
    for d in range(1, n):
        to = wrap(a + d, n)
        q_recv.append(go(remote(Q.at[to], RQ.at[d - 1], lat_of(to, b), t)))
    piece = Q[a]
    for d in range(1, n):
        q_recv[d - 1].wait_recv()
        piece = piece + RQ[d - 1]
    a_cols = pl.ds(pl.multiple_of(a * 128, 128), 128)
    db_cols = pl.ds(pl.multiple_of(c * width + a * 128, 128), 128)
    piece = piece + db_ref[:, db_cols] - XF[c, my_block, a_cols].astype(F32)
    RES[my_block, a_cols] = piece.astype(BF16)

    r_recv = []
    for d in range(1, n):
        to = wrap(a + d, n)
        r_recv.append(go(remote(RES.at[my_block, a_cols], RES.at[my_block, a_cols], lat_of(to, b), t)))
    for d in r_recv:
        d.wait_recv()
    ring_gather(RES)

    r_swap = go(remote(RES, RESF, partner, t))
    part = lax.dot_general(RES[...], WD[...], nt, preferred_element_type=F32)
    back = feature_sum(1, part)
    ag_s[...] = (0.5 * back * mask[...]).astype(BF16)
    ag_recv = []
    for d in range(1, X):
        ag_recv.append(go(remote(ag_s, ag_f.at[act_rows], L, wrap(t + d, X))))
    ag_f[act_rows, :] = ag_s[...]

    r_swap.wait_recv()
    x_swap.wait_recv()
    acts = act_f[:, act_cols]
    near = RES[...]
    far = RESF[...]
    near_g = (0.5 * lax.dot_general(acts, near, tn, preferred_element_type=F32)).astype(BF16)
    far_g = (0.5 * lax.dot_general(acts, far, tn, preferred_element_type=F32)).astype(BF16)
    gd_out[:, own_cols] = near_g
    gd_out[:, far_cols] = far_g
    pick_i = lax.broadcasted_iota(jnp.int32, (16, rows), 0)
    pick_j = lax.broadcasted_iota(jnp.int32, (16, rows), 1)
    pick = jnp.where((pick_i < own) & (pick_j == pick_i + L * own), 1.0, 0.0).astype(BF16)
    res_out[:, own_cols] = jnp.dot(pick, near, preferred_element_type=F32)[:own].astype(BF16)
    res_out[:, far_cols] = jnp.dot(pick, far, preferred_element_type=F32)[:own].astype(BF16)
    for d in pre_recv:
        d.wait_recv()
    pre_out[...] = pre_f[...]

    for d in ag_recv:
        d.wait_recv()
    grads = ag_f[...]
    for h in (0, 1):
        ge_out[:, h * width : (h + 1) * width] = lax.dot_general(
            grads, XF[h], tn, preferred_element_type=F32
        ).astype(BF16)
    for d in sends:
        d.wait_send()


def shards(mesh, resid_stream, enc_weight, enc_bias, dec_weight, dec_bias, active_ids, active_count):
    own, width = resid_stream.shape
    lat = enc_weight.shape[0]
    dm = Dims(mesh, own, width, lat, active_ids.shape[1])
    n, rows, block, w = dm.n, dm.rows, dm.block, dm.width
    vmem = pl.BlockSpec(memory_space=pltpu.VMEM)
    hbm = pl.BlockSpec(memory_space=pl.ANY)
    copies = 160
    out = pl.pallas_call(
        functools.partial(kernel, dm),
        out_shape=(
            jax.ShapeDtypeStruct((rows, lat), F32),
            jax.ShapeDtypeStruct((own, width), BF16),
            jax.ShapeDtypeStruct((lat, width), BF16),
            jax.ShapeDtypeStruct((lat, width), BF16),
        ),
        in_specs=[vmem] * 5 + [hbm] * 2,
        out_specs=(vmem,) * 4,
        scratch_shapes=[
            pltpu.VMEM((2, dm.flat, 128), F32),
            pltpu.VMEM((2 * n * dm.flat, 128), F32),
            pltpu.VMEM((rows, w), BF16),
            pltpu.VMEM((2, rows, w), BF16),
            pltpu.VMEM((2 * lat, w), BF16),
            pltpu.VMEM((2 * lat, w), BF16),
            pltpu.VMEM((2, 2, rows, lat), F32),
            pltpu.VMEM((2, rows, lat), F32),
            pltpu.VMEM((2, rows, lat), F32),
            pltpu.VMEM((2, dm.X - 1, dm.chunk, lat), F32),
            pltpu.VMEM((dm.chunk, lat), F32),
            pltpu.VMEM((dm.chunk, lat), BF16),
            pltpu.VMEM((rows, 2 * lat), BF16),
            pltpu.VMEM((dm.chunk, lat), F32),
            pltpu.VMEM((rows, lat), F32),
            pltpu.VMEM((rows, w), F32),
            pltpu.VMEM((2, n // 2, block, w), F32),
            pltpu.VMEM((n, block, 128), F32),
            pltpu.VMEM((n - 1, block, 128), F32),
            pltpu.VMEM((rows, w), BF16),
            pltpu.VMEM((rows, w), BF16),
            pltpu.VMEM((dm.chunk, lat), BF16),
            pltpu.VMEM((rows, lat), BF16),
            pltpu.SemaphoreType.DMA((copies,)),
            pltpu.SemaphoreType.DMA((copies,)),
            pltpu.SemaphoreType.DMA((4,)),
        ],
        compiler_params=pltpu.CompilerParams(
            collective_id=0, has_side_effects=True, vmem_limit_bytes=48 * 1024 * 1024
        ),
    )(
        resid_stream,
        active_ids,
        active_count.reshape(1, rows),
        enc_bias.reshape(1, lat),
        dec_bias.reshape(1, width),
        enc_weight,
        dec_weight,
    )
    return tuple(out)


def solution(mesh):
    placed = (P("lat", "tok"), P("lat", "tok"), P("lat"), P("lat", "tok"), P("tok"), P(), P())
    return jax.shard_map(
        functools.partial(shards, mesh),
        mesh=mesh,
        in_specs=placed,
        out_specs=(P(None, "lat"), P("lat", "tok"), P("lat", "tok"), P("lat", "tok")),
        check_vma=False,
    )
```

time: 428 us -> 111 us (0.26)
  waiting for transfers between devices: 387 us -> 0 us
  Pallas kernels: 0 us -> 104 us
  between operations: 13.9 us -> 0.69 us
  other arithmetic: 10.2 us -> 0 us
  matrix products: 8.73 us -> 0 us
    psum x3 -> x0, waiting for transfers between devices: 295 us -> none  [the longest x1 206 us: shards(): lax.psum(jnp.dot(activations, dec_weight, preferred_element_type=jnp.floa...]
    pallas_call x0 -> x1, Pallas kernels: none -> 104 us  [shards(): pl.pallas_call(functools.partial(kernel, dm), out_shape=(jax.ShapeDtypeSt...]
    all_gather x1 -> x0, waiting for transfers between devices: 91.1 us -> none  [shards(): full_rows = lax.all_gather(resid_stream, 'lat', axis=0, tiled=True)]
    dot_general x5 -> x0, matrix products: 8.73 us -> none  [the longest x1 2.68 us: shards(): lax.dot_general(activations, residual_all, (((0,), (0,)), ((), ())), pref...]
    convert_element_type x3 -> x0, other arithmetic: 5.04 us -> none  [the longest x1 2.44 us: shards(): (rebuilt + dec_bias[None, :] - full_rows.astype(jnp.float32)).astype(jnp....]
  transfers between devices with their start and end apart: 4 -> 0, of which waited for: 4 -> 0; matrix products, arithmetic and copies ran while one was open for 2% -> 0% of each run, Pallas kernels for 0% -> 0%
where the time goes in v1:
time: 111 us
  Pallas kernels  104 us (94%)
  local copies, waits for them, and re-layouts  6.69 us (6%)
    pallas_call x1, Pallas kernels, shards(): pl.pallas_call(functools.partial(kernel, dm), out_shape=(jax.ShapeDtypeSt...  104 us
    unnamed x17, local copies, waits for them, and re-layouts  6.69 us

profile of v1, /device:TPU:1, one launch (start us, length us, event | category | flops | bytes accessed | tf_op | source)
XLA Modules:
  0.0 110.9 jit_solution(12483251596663030701)
XLA Ops:
  0.6 0.0 copy-start.5
  0.6 0.7 copy-done.5
  1.3 0.0 copy-start.2
  1.3 0.0 copy-start.3
  1.3 0.0 copy-start.4
  1.3 1.1 copy.11.ids_ref
  2.4 0.0 copy-done.2
  2.4 0.0 copy-done.3
  2.4 0.0 copy-done.4
  2.4 0.0 copy-start
  2.4 1.0 copy-done
  3.5 0.0 copy-start.1
  3.5 1.0 copy-done.1
  4.5 103.5 %shard_map.102 = (f32[384,128]{1,0:T(8,128)S(1)}, bf16[3,2048]{1,0:T(4,128)(2,1)S(1)}, bf16[128,2048]{1,0:T(8,128)(2,1)S(1)}, bf16[128,2048]{1,0:T(8,128)(2,1)S(1)}) custom-call(bf16[3,2048]{1,0:T(4,128)(2,1)S(1)} %copy-done.2, s32[384,64]{1,0:T(8,128)S(1)} %copy.11.ids_ref, s32[1,384]{1,0:T(1,128)S(1)} %reshape.17.cnt_ref, f32[1,128]{1,0:T(1,128)S(1)} %bitcast.3, ...), custom_call_target="tpu_custom_call" | custom-call | tf_op jit(solution)/shard_map/pallas_call | solution.py:354
  108.0 0.7 copy.16
  108.7 0.6 copy.17
  109.3 0.8 copy.18
  110.1 0.8 copy.19
  (1 shorter events, 0.0 us)
Async XLA Ops:
  0.6 0.7 copy-start.5
  1.3 1.1 copy-start.2
  1.3 1.1 copy-start.3
  1.3 1.1 copy-start.4
  2.4 1.0 copy-start
  3.5 1.0 copy-start.1

commit v2 on v1

v2 whole, which is shorter than its diff:
```python
import functools
import math

import jax
import jax.numpy as jnp
from jax import lax
from jax.experimental import pallas as pl
from jax.experimental.pallas import tpu as pltpu
from jax.sharding import PartitionSpec as P

F32 = jnp.float32
BF16 = jnp.bfloat16
MESH = pl.DeviceIdType.MESH


def divisor(limit, by):
    s = 16
    m = (1 << s) // by + 1
    assert all((i * m) >> s == i // by for i in range(limit))
    return m, s


class Dims:
    def __init__(self, mesh, rows_own, width, lat_dev, top_count):
        self.X = mesh.shape["tok"]
        self.n = math.isqrt(mesh.shape["lat"] // 2)
        assert self.n * self.n * 2 == mesh.shape["lat"]
        self.own = rows_own
        self.rows = rows_own * mesh.shape["lat"]
        self.block = self.rows // self.n
        self.width = width // 2
        self.lanes = self.width // 128
        self.flat = rows_own * self.lanes
        self.lat = lat_dev
        self.top = top_count
        self.chunk = self.rows // self.X
        self.parts = 4
        self.part_cols = self.width // self.parts


def kernel(
    dm,
    x_hbm, ids_hbm, cnt_hbm, eb_hbm, db_hbm, enc_ref, dec_ref,
    pre_f, res_out, gd_out, ag_f, XF,
    xs, ids_ref, cnt_ref, eb_ref, db_ref, F, R1, Xraw, WE, WD, PS, PR, SUM, RX, mask_all, mask, act_s, act_f, pre_s,
    T, RB, Q, RQ, RES, RESF, ag_s,
    send, recv, local,
):
    n, X, own, block, width, lanes, flat = dm.n, dm.X, dm.own, dm.block, dm.width, dm.lanes, dm.flat
    rows, lat, chunk = dm.rows, dm.lat, dm.chunk
    parts, part_cols = dm.parts, dm.part_cols
    depth = n // 2
    L = lax.axis_index("lat")
    t = lax.axis_index("tok")
    c = lax.rem(L, 2)
    chip = L // 2
    y = lax.rem(chip, n)
    z = chip // n
    a = y + c * (z - y)
    b = z + c * (y - z)
    partner = L + 1 - 2 * c

    def lat_of(ap, bp):
        yy = ap + c * (bp - ap)
        zz = bp + c * (ap - bp)
        return (zz * n + yy) * 2 + c

    count = {"copy": 0, "local": 0}
    sends = []

    def wrap(v, m):
        return lax.rem(v + 2 * m, m)

    def remote(src, dst, lat_id, tok_id, recv_index=None):
        k = count["copy"]
        count["copy"] += 1
        r = k if recv_index is None else recv_index
        d = pltpu.make_async_remote_copy(
            src_ref=src, dst_ref=dst, send_sem=send.at[k], recv_sem=recv.at[r],
            device_id=(lat_id, tok_id), device_id_type=MESH,
        )
        return d

    def go(d):
        d.start()
        sends.append(d)
        return d

    def copy_local(src, dst):
        k = count["local"]
        count["local"] += 1
        d = pltpu.make_async_copy(src, dst, local.at[k])
        d.start()
        return d

    x_in = copy_local(x_hbm, xs)

    barrier = pltpu.get_barrier_semaphore()
    heard = 0

    def greet(lat_id, tok_id):
        pl.semaphore_signal(barrier, inc=1, device_id=(lat_id, tok_id), device_id_type=MESH)

    greet(partner, t)
    heard += 1
    for d in range(1, n):
        for other in (0, 1):
            dev = lat_of(wrap(a + d, n), b)
            greet(dev + other * (1 - 2 * c), t)
    heard += 2 * (n - 1)
    for s in (1, -1):
        greet(lat_of(a, wrap(b + s, n)), t)
    heard += 2
    for d in range(1, X):
        for dev in (L, partner):
            greet(dev, wrap(t + d, X))
    heard += 2 * (X - 1)

    x_in.wait()
    xv = xs[...].astype(F32)
    for r in range(own):
        for j in range(2 * lanes):
            F[j // lanes, r * lanes + j % lanes : r * lanes + j % lanes + 1, :] = xv[
                r : r + 1, j * 128 : (j + 1) * 128
            ]

    small_in = [
        copy_local(ids_hbm, ids_ref),
        copy_local(cnt_hbm, cnt_ref),
        copy_local(eb_hbm, eb_ref),
        copy_local(db_hbm, db_ref),
    ]
    pl.semaphore_wait(barrier, heard)

    recv1 = count["copy"]
    count["copy"] += 2 * n

    def slot1(pos, core):
        return pl.ds(pl.multiple_of((pos * 2 + core) * flat, 8), flat)

    go(remote(F.at[1 - c], R1.at[slot1(y + (1 - c) * (z - y), c)], partner, t, recv1 + c))
    for d in range(1, n):
        for h in (0, 1):
            pos = (y, z)[h]
            yy = wrap(y + d, n) if h == 0 else y
            zz = wrap(z + d, n) if h == 1 else z
            go(remote(F.at[h], R1.at[slot1(pos, c)], (zz * n + yy) * 2 + h, t, recv1 + 2 * d + c))
    mine = F[c]
    R1[slot1(a, c), :] = mine

    own_cols = pl.ds(pl.multiple_of(c * width, 128), width)
    far_cols = pl.ds(pl.multiple_of((1 - c) * width, 128), width)
    own_lats = pl.ds(pl.multiple_of(c * lat, lat), lat)
    w_local = [copy_local(enc_ref.at[:, own_cols], WE.at[own_lats]), copy_local(dec_ref.at[:, own_cols], WD.at[own_lats])]
    w_remote = [
        go(remote(enc_ref.at[:, far_cols], WE.at[own_lats], partner, t)),
        go(remote(dec_ref.at[:, far_cols], WD.at[own_lats], partner, t)),
    ]

    my_rows = pl.ds(pl.multiple_of(t * chunk, 8), chunk)
    for d in small_in:
        d.wait()
    k_i = lax.broadcasted_iota(jnp.int32, (dm.top, rows), 0)
    local_ids = jnp.where(k_i < jnp.broadcast_to(cnt_ref[...].reshape(1, rows), (dm.top, rows)), ids_ref[...] - L * lat, -1)
    lat_i = lax.broadcasted_iota(jnp.int32, (lat, rows), 0)
    m = jnp.zeros((lat, rows), F32)
    for k in range(dm.top):
        m = jnp.where(local_ids[k : k + 1, :] == lat_i, 1.0, m)
    mask_all[...] = m.T
    mask[...] = mask_all[my_rows, :]

    m1, s1 = divisor(rows, block)
    m2, s2 = divisor(block, block // n)
    i0 = lax.broadcasted_iota(jnp.int32, (rows, rows), 0)
    i1 = lax.broadcasted_iota(jnp.int32, (rows, rows), 1)
    hi = (i0 * m1) >> s1
    rest = i0 - hi * block
    mid = (rest * m2) >> s2
    low = rest - mid * (block // n)
    order = i0 + c * (mid * block + hi * (block // n) + low - i0)
    perm = jnp.where(order == i1, 1.0, 0.0).astype(BF16)

    def remote_wait(index):
        pltpu.make_async_remote_copy(
            src_ref=F.at[0], dst_ref=R1.at[pl.ds(0, flat)], send_sem=send.at[0], recv_sem=recv.at[index],
            device_id=(partner, t), device_id_type=MESH,
        ).wait_recv()

    remote_wait(recv1 + 1 - c)
    for d in range(1, n):
        for core in (0, 1):
            remote_wait(recv1 + 2 * d + core)
    my_block = pl.ds(pl.multiple_of(b * block, 16), block)
    for j in range(lanes):
        at = j * 128 % part_cols
        Xraw[j * 128 // part_cols, my_block, at : at + 128] = R1[pl.ds(j, block, stride=lanes), :].astype(BF16)

    def far_parts(way):
        return range(parts // 2) if way == 1 else range(parts // 2, parts)

    def near_parts(way):
        return far_parts(-way)

    def block_rows(pos):
        return pl.ds(pl.multiple_of(pos * block, 16), block)

    def ring_gather(buf):
        flying = {}
        for s in range(1, depth + 1):
            for i in range(parts):
                for way in (1, -1):
                    h = (*far_parts(way), *near_parts(way))[i]
                    if s > 1:
                        flying[way, s - 1, h].wait_recv()
                    if s < depth or h in far_parts(way):
                        piece = buf.at[h, block_rows(wrap(b - way * (s - 1), n))]
                        flying[way, s, h] = go(remote(piece, piece, lat_of(a, wrap(b + way, n)), t))
        for i in range(parts // 2):
            for way in (1, -1):
                flying[way, depth, far_parts(way)[i]].wait_recv()

    ring_gather(Xraw)

    for w in w_local:
        w.wait()
    for w in w_remote:
        w.wait_recv()

    for h in range(parts):
        XF[c, :, h * part_cols : (h + 1) * part_cols] = jnp.dot(perm, Xraw[h], preferred_element_type=F32).astype(BF16)
    x_swap = go(remote(XF.at[c], XF.at[c], partner, t))

    order = sorted(range(X), key=lambda d: -min(d, X - d))

    def feature_sum(u, lhs, rhs):
        swap = {}
        arrive = {}
        for d in order:
            part = lax.dot_general(
                lhs(pl.ds(pl.multiple_of(wrap(t + d, X) * chunk, 16), chunk)), rhs, nt, preferred_element_type=F32
            )
            PS[u, d, 0] = part[:, :lat]
            PS[u, d, 1] = part[:, lat:]
            swap[d] = go(remote(PS.at[u, d, 1 - c], PR.at[u, d], partner, t))
        for d in order:
            swap[d].wait_recv()
            SUM[u, d] = PS[u, d, c] + PR[u, d]
            if d:
                arrive[d] = go(remote(SUM.at[u, d], RX.at[u, d - 1], L, wrap(t + d, X)))
        total = SUM[u, 0]
        for d in sorted(arrive, key=lambda d: min(d, X - d)):
            arrive[d].wait_recv()
            total = total + RX[u, d - 1]
        return total

    nt = (((1,), (1,)), ((), ()))
    tn = (((0,), (0,)), ((), ()))
    pre = feature_sum(0, lambda r: XF[c, r, :], WE[...]) + eb_ref[...]
    act_s[...] = (pre * mask[...]).astype(BF16)
    pre_s[...] = pre
    act_rows = pl.ds(pl.multiple_of(t * chunk, 16), chunk)
    act_cols = pl.ds(pl.multiple_of(c * lat, lat), lat)
    act_recv = []
    for d in range(1, X):
        to = wrap(t + d, X)
        for swap in (0, 1):
            dev = L + swap * (1 - 2 * c)
            act_recv.append(go(remote(act_s, act_f.at[act_rows, act_cols], dev, to)))
    act_recv.append(go(remote(act_s, act_f.at[act_rows, act_cols], partner, t)))
    act_f[act_rows, act_cols] = act_s[...]
    pre_recv = []
    for d in range(1, X):
        pre_recv.append(go(remote(pre_s, pre_f.at[my_rows], L, wrap(t + d, X))))
    pre_f[my_rows, :] = pre
    for d in act_recv:
        d.wait_recv()

    def rebuild(pos):
        at = block_rows(pos)
        value = jnp.dot(act_f[at, :], WD[...], preferred_element_type=F32)
        for h in range(parts):
            T[h, at, :] = value[:, h * part_cols : (h + 1) * part_cols]

    flying = {}

    def ring_reduce_hop(i):
        for k in range(parts):
            for way in (1, -1):
                far = k < parts // 2
                h = (*far_parts(way), *near_parts(way))[k]
                hops = depth if far else depth - 1
                if i > hops:
                    continue
                at = block_rows(wrap(b + way * (hops + 1 - i), n))
                w = 0 if way == 1 else 1
                if i > 1:
                    flying[way, i - 1, h].wait_recv()
                    T[h, at, :] = T[h, at, :] + RB[w, i - 2, h]
                flying[way, i, h] = go(remote(T.at[h, at], RB.at[w, i - 1, h], lat_of(a, wrap(b + way, n)), t))

    rebuild(wrap(b + depth, n))
    for k in range(depth - 1, 0, -1):
        rebuild(wrap(b + k, n))
        rebuild(wrap(b - k, n))
        if k == depth - 1:
            ring_reduce_hop(1)
    rebuild(b)
    for i in range(2, depth + 1):
        ring_reduce_hop(i)
    for h in (*near_parts(1), *far_parts(1)):
        q = T[h, my_block, :]
        for way in (1, -1):
            hops = depth if h in far_parts(way) else depth - 1
            flying[way, hops, h].wait_recv()
            q = q + RB[0 if way == 1 else 1, hops - 1, h]
        for j in range(part_cols // 128):
            Q[h * (part_cols // 128) + j] = q[:, j * 128 : (j + 1) * 128]
    q_recv = []
    for d in range(1, n):
        to = wrap(a + d, n)
        q_recv.append(go(remote(Q.at[to], RQ.at[d - 1], lat_of(to, b), t)))
    piece = Q[a]
    for d in range(1, n):
        q_recv[d - 1].wait_recv()
        piece = piece + RQ[d - 1]
    a_cols = pl.ds(pl.multiple_of(a * 128, 128), 128)
    db_cols = pl.ds(pl.multiple_of(c * width + a * 128, 128), 128)
    piece = piece + db_ref[:, db_cols] - XF[c, my_block, a_cols].astype(F32)
    per = part_cols // 128
    res_piece = RES.at[a // per, my_block, pl.ds(pl.multiple_of(lax.rem(a, per) * 128, 128), 128)]
    res_piece[...] = piece.astype(BF16)

    r_recv = []
    for d in range(1, n):
        to = wrap(a + d, n)
        r_recv.append(go(remote(res_piece, res_piece, lat_of(to, b), t)))
    for d in r_recv:
        d.wait_recv()
    ring_gather(RES)

    r_swap = go(remote(RES, RESF, partner, t))
    back = feature_sum(1, lambda r: jnp.concatenate([RES[h, r, :] for h in range(parts)], axis=1), WD[...])
    ag_s[...] = (0.5 * back * mask[...]).astype(BF16)
    ag_recv = []
    for d in range(1, X):
        ag_recv.append(go(remote(ag_s, ag_f.at[act_rows], L, wrap(t + d, X))))
    ag_f[act_rows, :] = ag_s[...]

    r_swap.wait_recv()
    x_swap.wait_recv()
    acts = act_f[:, act_cols]
    pick_i = lax.broadcasted_iota(jnp.int32, (16, rows), 0)
    pick_j = lax.broadcasted_iota(jnp.int32, (16, rows), 1)
    pick = jnp.where((pick_i < own) & (pick_j == pick_i + L * own), 1.0, 0.0).astype(BF16)
    for core, buf in ((c, RES), (1 - c, RESF)):
        for h in range(parts):
            cols = pl.ds(pl.multiple_of(core * width + h * part_cols, 128), part_cols)
            gd_out[:, cols] = (0.5 * lax.dot_general(acts, buf[h], tn, preferred_element_type=F32)).astype(BF16)
            res_out[:, cols] = jnp.dot(pick, buf[h], preferred_element_type=F32)[:own].astype(BF16)
    for d in pre_recv:
        d.wait_recv()
    for d in ag_recv:
        d.wait_recv()
    for d in sends:
        d.wait_send()


def finish(pre_ref, res_ref, gd_ref, ag_ref, xf_ref, pre_out, res_out, ge_out, gd_out, ge_s, sems):
    moves = [
        pltpu.make_async_copy(pre_ref, pre_out, sems.at[0]),
        pltpu.make_async_copy(res_ref, res_out, sems.at[1]),
        pltpu.make_async_copy(gd_ref, gd_out, sems.at[2]),
    ]
    for d in moves:
        d.start()
    width = ge_s.shape[2]
    grads = ag_ref[...]
    for h in (0, 1):
        ge_s[h] = lax.dot_general(
            grads, xf_ref[h], (((0,), (0,)), ((), ())), preferred_element_type=F32
        ).astype(BF16)
        d = pltpu.make_async_copy(ge_s.at[h], ge_out.at[:, pl.ds(h * width, width)], sems.at[3 + h])
        d.start()
        moves.append(d)
    for d in moves:
        d.wait()


def shards(mesh, resid_stream, enc_weight, enc_bias, dec_weight, dec_bias, active_ids, active_count):
    own, width = resid_stream.shape
    lat = enc_weight.shape[0]
    dm = Dims(mesh, own, width, lat, active_ids.shape[1])
    n, rows, block, w = dm.n, dm.rows, dm.block, dm.width
    vmem = pl.BlockSpec(memory_space=pltpu.VMEM)
    hbm = pl.BlockSpec(memory_space=pltpu.HBM)
    copies = 288
    pre, res, gd, ag, xf = pl.pallas_call(
        functools.partial(kernel, dm),
        out_shape=(
            jax.ShapeDtypeStruct((rows, lat), F32),
            jax.ShapeDtypeStruct((own, width), BF16),
            jax.ShapeDtypeStruct((lat, width), BF16),
            jax.ShapeDtypeStruct((rows, lat), BF16),
            jax.ShapeDtypeStruct((2, rows, w), BF16),
        ),
        in_specs=[hbm] * 7,
        out_specs=(vmem,) * 5,
        scratch_shapes=[
            pltpu.VMEM((own, width), BF16),
            pltpu.VMEM((dm.top, rows), jnp.int32),
            pltpu.VMEM((rows,), jnp.int32),
            pltpu.VMEM((1, lat), F32),
            pltpu.VMEM((1, width), F32),
            pltpu.VMEM((2, dm.flat, 128), F32),
            pltpu.VMEM((2 * n * dm.flat, 128), F32),
            pltpu.VMEM((dm.parts, rows, dm.part_cols), BF16),
            pltpu.VMEM((2 * lat, w), BF16),
            pltpu.VMEM((2 * lat, w), BF16),
            pltpu.VMEM((2, dm.X, 2, dm.chunk, lat), F32),
            pltpu.VMEM((2, dm.X, dm.chunk, lat), F32),
            pltpu.VMEM((2, dm.X, dm.chunk, lat), F32),
            pltpu.VMEM((2, dm.X - 1, dm.chunk, lat), F32),
            pltpu.VMEM((rows, lat), F32),
            pltpu.VMEM((dm.chunk, lat), F32),
            pltpu.VMEM((dm.chunk, lat), BF16),
            pltpu.VMEM((rows, 2 * lat), BF16),
            pltpu.VMEM((dm.chunk, lat), F32),
            pltpu.VMEM((dm.parts, rows, dm.part_cols), F32),
            pltpu.VMEM((2, n // 2, dm.parts, block, dm.part_cols), F32),
            pltpu.VMEM((n, block, 128), F32),
            pltpu.VMEM((n - 1, block, 128), F32),
            pltpu.VMEM((dm.parts, rows, dm.part_cols), BF16),
            pltpu.VMEM((dm.parts, rows, dm.part_cols), BF16),
            pltpu.VMEM((dm.chunk, lat), BF16),
            pltpu.SemaphoreType.DMA((copies,)),
            pltpu.SemaphoreType.DMA((copies,)),
            pltpu.SemaphoreType.DMA((8,)),
        ],
        compiler_params=pltpu.CompilerParams(
            collective_id=0, has_side_effects=True, vmem_limit_bytes=48 * 1024 * 1024
        ),
    )(
        *(
            pltpu.with_memory_space_constraint(v, pltpu.HBM)
            for v in (
                resid_stream,
                active_ids.T,
                active_count,
                enc_bias.reshape(1, lat),
                dec_bias.reshape(1, width),
                enc_weight,
                dec_weight,
            )
        )
    )
    return pl.pallas_call(
        finish,
        out_shape=(
            jax.ShapeDtypeStruct((rows, lat), F32),
            jax.ShapeDtypeStruct((own, width), BF16),
            jax.ShapeDtypeStruct((lat, width), BF16),
            jax.ShapeDtypeStruct((lat, width), BF16),
        ),
        in_specs=[vmem] * 5,
        out_specs=(hbm,) * 4,
        scratch_shapes=[pltpu.VMEM((2, lat, w), BF16), pltpu.SemaphoreType.DMA((5,))],
        compiler_params=pltpu.CompilerParams(vmem_limit_bytes=4 * 1024 * 1024),
    )(pre, res, gd, ag, xf)


def solution(mesh):
    placed = (P("lat", "tok"), P("lat", "tok"), P("lat"), P("lat", "tok"), P("tok"), P(), P())
    return jax.shard_map(
        functools.partial(shards, mesh),
        mesh=mesh,
        in_specs=placed,
        out_specs=(P(None, "lat"), P("lat", "tok"), P("lat", "tok"), P("lat", "tok")),
        check_vma=False,
    )
```

time: 111 us -> 103 us (0.928)
  local copies, waits for them, and re-layouts: 6.69 us -> 0 us
  Pallas kernels: 104 us -> 102 us
    unnamed x17 -> x0, local copies, waits for them, and re-layouts: 6.69 us -> none
    pallas_call x1, Pallas kernels: 104 us -> 100 us  [shards(): pl.pallas_call(functools.partial(kernel, dm), out_shape=(jax.ShapeDtypeSt...]
    pallas_call x0 -> x1, Pallas kernels: none -> 1.21 us  [shards(): pl.pallas_call(finish, out_shape=(jax.ShapeDtypeStruct((rows, lat), F32),...]
where the time goes in v2:
time: 103 us; the launch traced here: 102 us
  Pallas kernels  102 us (99%)
    pallas_call x1, Pallas kernels, shards(): pl.pallas_call(functools.partial(kernel, dm), out_shape=(jax.ShapeDtypeSt...  100 us

profile of v2, /device:TPU:1, one launch (start us, length us, event | category | flops | bytes accessed | tf_op | source)
XLA Modules:
  0.0 102.3 jit_solution(7188876486782106071)
XLA Ops:
  0.6 100.5 %shard_map.102 = (f32[384,128]{1,0:T(8,128)S(1)}, bf16[3,2048]{1,0:T(4,128)(2,1)S(1)}, bf16[128,2048]{1,0:T(8,128)(2,1)S(1)}, bf16[384,128]{1,0:T(8,128)(2,1)S(1)}, bf16[2,384,1024]{2,1,0:T(8,128)(2,1)S(1)}) custom-call(bf16[3,2048]{1,0:T(4,128)(2,1)} %x_hbm.1, s32[64,384]{1,0:T(8,128)} %bitcast.3, s32[384]{0:T(512)} %cnt_hbm.1, f32[1,128]{1,0:T(1,128)} %bitcast.5, ...), custom_call_target="tpu_custom_call" | custom-call | tf_op jit(solution)/shard_map/pallas_call | solution.py:397
  101.1 1.2 %shard_map.103 = (f32[384,128]{1,0:T(8,128)}, bf16[3,2048]{1,0:T(4,128)(2,1)}, bf16[128,2048]{1,0:T(8,128)(2,1)}, bf16[128,2048]{1,0:T(8,128)(2,1)}) custom-call(f32[384,128]{1,0:T(8,128)S(1)} %get-tuple-element.9.pre_ref, bf16[3,2048]{1,0:T(4,128)(2,1)S(1)} %get-tuple-element.10.res_ref, bf16[128,2048]{1,0:T(8,128)(2,1)S(1)} %get-tuple-element.11.gd_ref, ...), custom_call_target="tpu_custom_call" | custom-call | tf_op jit(solution)/shard_map/pallas_call | solution.py:456

commit v3 on v2

--- a/solution.py
+++ b/solution.py
@@ -13,18 +13,11 @@
 MESH = pl.DeviceIdType.MESH
 
 
-def divisor(limit, by):
-    s = 16
-    m = (1 << s) // by + 1
-    assert all((i * m) >> s == i // by for i in range(limit))
-    return m, s
-
-
 class Dims:
     def __init__(self, mesh, rows_own, width, lat_dev, top_count):
         self.X = mesh.shape["tok"]
         self.n = math.isqrt(mesh.shape["lat"] // 2)
-        assert self.n * self.n * 2 == mesh.shape["lat"]
+        assert self.n == 8 and self.n * self.n * 2 == mesh.shape["lat"]
         self.own = rows_own
         self.rows = rows_own * mesh.shape["lat"]
         self.block = self.rows // self.n
@@ -42,7 +35,7 @@
     dm,
     x_hbm, ids_hbm, cnt_hbm, eb_hbm, db_hbm, enc_ref, dec_ref,
     pre_f, res_out, gd_out, ag_f, XF,
-    xs, ids_ref, cnt_ref, eb_ref, db_ref, F, R1, Xraw, WE, WD, PS, PR, SUM, RX, mask_all, mask, act_s, act_f, pre_s,
+    xs, ids_ref, cnt_ref, eb_ref, db_ref, F32S, F, X3, XL, WE, WD, PS, PR, SUM, RX, mask_all, mask, act_s, act_f, pre_s,
     T, RB, Q, RQ, RES, RESF, ag_s,
     send, recv, local,
 ):
@@ -108,9 +101,9 @@
             dev = lat_of(wrap(a + d, n), b)
             greet(dev + other * (1 - 2 * c), t)
     heard += 2 * (n - 1)
-    for s in (1, -1):
+    for s in (1, -1, 2, -2):
         greet(lat_of(a, wrap(b + s, n)), t)
-    heard += 2
+    heard += 4
     for d in range(1, X):
         for dev in (L, partner):
             greet(dev, wrap(t + d, X))
@@ -120,9 +113,10 @@
     xv = xs[...].astype(F32)
     for r in range(own):
         for j in range(2 * lanes):
-            F[j // lanes, r * lanes + j % lanes : r * lanes + j % lanes + 1, :] = xv[
-                r : r + 1, j * 128 : (j + 1) * 128
-            ]
+            at = r * lanes + j % lanes
+            F32S[j // lanes, at : at + 1, :] = xv[r : r + 1, j * 128 : (j + 1) * 128]
+    for h in (0, 1):
+        F[h] = F32S[h].reshape(own, lanes, 128).astype(BF16)
 
     small_in = [
         copy_local(ids_hbm, ids_ref),
@@ -135,18 +129,14 @@
     recv1 = count["copy"]
     count["copy"] += 2 * n
 
-    def slot1(pos, core):
-        return pl.ds(pl.multiple_of((pos * 2 + core) * flat, 8), flat)
-
-    go(remote(F.at[1 - c], R1.at[slot1(y + (1 - c) * (z - y), c)], partner, t, recv1 + c))
+    my_x = X3.at[pl.ds(L * own, own)]
+    go(remote(F.at[1 - c], my_x, partner, t, recv1 + c))
     for d in range(1, n):
         for h in (0, 1):
-            pos = (y, z)[h]
             yy = wrap(y + d, n) if h == 0 else y
             zz = wrap(z + d, n) if h == 1 else z
-            go(remote(F.at[h], R1.at[slot1(pos, c)], (zz * n + yy) * 2 + h, t, recv1 + 2 * d + c))
-    mine = F[c]
-    R1[slot1(a, c), :] = mine
+            go(remote(F.at[h], my_x, (zz * n + yy) * 2 + h, t, recv1 + 2 * d + c))
+    my_x[...] = F[c]
 
     own_cols = pl.ds(pl.multiple_of(c * width, 128), width)
     far_cols = pl.ds(pl.multiple_of((1 - c) * width, 128), width)
@@ -169,32 +159,6 @@
     mask_all[...] = m.T
     mask[...] = mask_all[my_rows, :]
 
-    m1, s1 = divisor(rows, block)
-    m2, s2 = divisor(block, block // n)
-    i0 = lax.broadcasted_iota(jnp.int32, (rows, rows), 0)
-    i1 = lax.broadcasted_iota(jnp.int32, (rows, rows), 1)
-    hi = (i0 * m1) >> s1
-    rest = i0 - hi * block
-    mid = (rest * m2) >> s2
-    low = rest - mid * (block // n)
-    order = i0 + c * (mid * block + hi * (block // n) + low - i0)
-    perm = jnp.where(order == i1, 1.0, 0.0).astype(BF16)
-
-    def remote_wait(index):
-        pltpu.make_async_remote_copy(
-            src_ref=F.at[0], dst_ref=R1.at[pl.ds(0, flat)], send_sem=send.at[0], recv_sem=recv.at[index],
-            device_id=(partner, t), device_id_type=MESH,
-        ).wait_recv()
-
-    remote_wait(recv1 + 1 - c)
-    for d in range(1, n):
-        for core in (0, 1):
-            remote_wait(recv1 + 2 * d + core)
-    my_block = pl.ds(pl.multiple_of(b * block, 16), block)
-    for j in range(lanes):
-        at = j * 128 % part_cols
-        Xraw[j * 128 // part_cols, my_block, at : at + 128] = R1[pl.ds(j, block, stride=lanes), :].astype(BF16)
-
     def far_parts(way):
         return range(parts // 2) if way == 1 else range(parts // 2, parts)
 
@@ -204,30 +168,63 @@
     def block_rows(pos):
         return pl.ds(pl.multiple_of(pos * block, 16), block)
 
-    def ring_gather(buf):
-        flying = {}
-        for s in range(1, depth + 1):
-            for i in range(parts):
-                for way in (1, -1):
-                    h = (*far_parts(way), *near_parts(way))[i]
-                    if s > 1:
-                        flying[way, s - 1, h].wait_recv()
-                    if s < depth or h in far_parts(way):
-                        piece = buf.at[h, block_rows(wrap(b - way * (s - 1), n))]
-                        flying[way, s, h] = go(remote(piece, piece, lat_of(a, wrap(b + way, n)), t))
-        for i in range(parts // 2):
+    my_block = block_rows(b)
+
+    def spread(piece, ready):
+        by_distance = sorted(range(n), key=lambda d: min(d, n - d))
+        first, second = {}, {}
+
+        def push(offset, d, pos):
+            ref = piece(wrap(a + d, n), wrap(pos, n))
+            return go(remote(ref, ref, lat_of(a, wrap(b + offset, n)), t))
+
+        def level1(d):
+            ready(d)
+            for offset in (2, -2, 1, -1):
+                first[offset, d] = push(offset, d, b)
+
+        def level2(k, d):
             for way in (1, -1):
-                flying[way, depth, far_parts(way)[i]].wait_recv()
-
-    ring_gather(Xraw)
+                first[2 * way, d].wait_recv()
+                if (k % 2 == 0) == (way == 1):
+                    second[2 * way, d] = push(2 * way, d, b - 2 * way)
+                second[way, d] = push(way, d, b - 2 * way)
+
+        for d in by_distance[:5]:
+            level1(d)
+        level2(0, by_distance[0])
+        for d in by_distance[5:]:
+            level1(d)
+        for k, d in enumerate(by_distance):
+            if k:
+                level2(k, d)
+        for d in by_distance:
+            first[1, d].wait_recv()
+            first[-1, d].wait_recv()
+        for got in second.values():
+            got.wait_recv()
+
+    def x_ready(d):
+        back = (n - d) % n
+        for core in (0, 1) if d else (1 - c,):
+            pltpu.make_async_remote_copy(
+                src_ref=F.at[0], dst_ref=X3.at[pl.ds(0, own)], send_sem=send.at[0],
+                recv_sem=recv.at[recv1 + 2 * back + core], device_id=(partner, t), device_id_type=MESH,
+            ).wait_recv()
+
+    def x_piece(ap, bp):
+        return X3.at[pl.ds((lat_of(ap, bp) - c) * own, 2 * own)]
+
+    spread(x_piece, x_ready)
 
     for w in w_local:
         w.wait()
     for w in w_remote:
         w.wait_recv()
 
-    for h in range(parts):
-        XF[c, :, h * part_cols : (h + 1) * part_cols] = jnp.dot(perm, Xraw[h], preferred_element_type=F32).astype(BF16)
+    XL[...] = X3[...].astype(F32).reshape(rows * lanes, 128)
+    for j in range(lanes):
+        XF[c, :, j * 128 : (j + 1) * 128] = XL[pl.ds(j, rows, stride=lanes), :].astype(BF16)
     x_swap = go(remote(XF.at[c], XF.at[c], partner, t))
 
     order = sorted(range(X), key=lambda d: -min(d, X - d))
@@ -326,20 +323,24 @@
     a_cols = pl.ds(pl.multiple_of(a * 128, 128), 128)
     db_cols = pl.ds(pl.multiple_of(c * width + a * 128, 128), 128)
     piece = piece + db_ref[:, db_cols] - XF[c, my_block, a_cols].astype(F32)
-    per = part_cols // 128
-    res_piece = RES.at[a // per, my_block, pl.ds(pl.multiple_of(lax.rem(a, per) * 128, 128), 128)]
-    res_piece[...] = piece.astype(BF16)
-
-    r_recv = []
+    RES[a, my_block, :] = piece.astype(BF16)
+
+    def res_piece(ap, bp):
+        return RES.at[ap, block_rows(bp)]
+
+    r_recv = {}
     for d in range(1, n):
-        to = wrap(a + d, n)
-        r_recv.append(go(remote(res_piece, res_piece, lat_of(to, b), t)))
-    for d in r_recv:
-        d.wait_recv()
-    ring_gather(RES)
+        ref = res_piece(a, b)
+        r_recv[n - d] = go(remote(ref, ref, lat_of(wrap(a + d, n), b), t))
+
+    def res_ready(d):
+        if d:
+            r_recv[d].wait_recv()
+
+    spread(res_piece, res_ready)
 
     r_swap = go(remote(RES, RESF, partner, t))
-    back = feature_sum(1, lambda r: jnp.concatenate([RES[h, r, :] for h in range(parts)], axis=1), WD[...])
+    back = feature_sum(1, lambda r: jnp.concatenate([RES[j, r, :] for j in range(lanes)], axis=1), WD[...])
     ag_s[...] = (0.5 * back * mask[...]).astype(BF16)
     ag_recv = []
     for d in range(1, X):
@@ -352,11 +353,10 @@
     pick_i = lax.broadcasted_iota(jnp.int32, (16, rows), 0)
     pick_j = lax.broadcasted_iota(jnp.int32, (16, rows), 1)
     pick = jnp.where((pick_i < own) & (pick_j == pick_i + L * own), 1.0, 0.0).astype(BF16)
-    for core, buf in ((c, RES), (1 - c, RESF)):
-        for h in range(parts):
-            cols = pl.ds(pl.multiple_of(core * width + h * part_cols, 128), part_cols)
-            gd_out[:, cols] = (0.5 * lax.dot_general(acts, buf[h], tn, preferred_element_type=F32)).astype(BF16)
-            res_out[:, cols] = jnp.dot(pick, buf[h], preferred_element_type=F32)[:own].astype(BF16)
+    for cols, buf in ((own_cols, RES), (far_cols, RESF)):
+        value = jnp.concatenate([buf[j] for j in range(lanes)], axis=1)
+        gd_out[:, cols] = (0.5 * lax.dot_general(acts, value, tn, preferred_element_type=F32)).astype(BF16)
+        res_out[:, cols] = jnp.dot(pick, value, preferred_element_type=F32)[:own].astype(BF16)
     for d in pre_recv:
         d.wait_recv()
     for d in ag_recv:
@@ -412,8 +412,9 @@
             pltpu.VMEM((1, lat), F32),
             pltpu.VMEM((1, width), F32),
             pltpu.VMEM((2, dm.flat, 128), F32),
-            pltpu.VMEM((2 * n * dm.flat, 128), F32),
-            pltpu.VMEM((dm.parts, rows, dm.part_cols), BF16),
+            pltpu.VMEM((2, own, dm.lanes, 128), BF16),
+            pltpu.VMEM((rows, dm.lanes, 128), BF16),
+            pltpu.VMEM((rows * dm.lanes, 128), F32),
             pltpu.VMEM((2 * lat, w), BF16),
             pltpu.VMEM((2 * lat, w), BF16),
             pltpu.VMEM((2, dm.X, 2, dm.chunk, lat), F32),
@@ -429,8 +430,8 @@
             pltpu.VMEM((2, n // 2, dm.parts, block, dm.part_cols), F32),
             pltpu.VMEM((n, block, 128), F32),
             pltpu.VMEM((n - 1, block, 128), F32),
-            pltpu.VMEM((dm.parts, rows, dm.part_cols), BF16),
-            pltpu.VMEM((dm.parts, rows, dm.part_cols), BF16),
+            pltpu.VMEM((dm.lanes, rows, 128), BF16),
+            pltpu.VMEM((dm.lanes, rows, 128), BF16),
             pltpu.VMEM((dm.chunk, lat), BF16),
             pltpu.SemaphoreType.DMA((copies,)),
             pltpu.SemaphoreType.DMA((copies,)),

time: 103 us -> 93.7 us (0.910)
  Pallas kernels: 102 us -> 92.9 us
    pallas_call x1, Pallas kernels: 100 us -> 91.7 us  [shards(): pl.pallas_call(functools.partial(kernel, dm), out_shape=(jax.ShapeDtypeSt...]
where the time goes in v3:
time: 93.7 us; the launch traced here: 93.5 us
  Pallas kernels  92.9 us (99%)
    pallas_call x1, Pallas kernels, shards(): pl.pallas_call(functools.partial(kernel, dm), out_shape=(jax.ShapeDtypeSt...  91.7 us

profile of v3, /device:TPU:1, one launch (start us, length us, event | category | flops | bytes accessed | tf_op | source)
XLA Modules:
  0.0 93.5 jit_solution(10120306421589998810)
XLA Ops:
  0.6 91.7 %shard_map.102 = (f32[384,128]{1,0:T(8,128)S(1)}, bf16[3,2048]{1,0:T(4,128)(2,1)S(1)}, bf16[128,2048]{1,0:T(8,128)(2,1)S(1)}, bf16[384,128]{1,0:T(8,128)(2,1)S(1)}, bf16[2,384,1024]{2,1,0:T(8,128)(2,1)S(1)}) custom-call(bf16[3,2048]{1,0:T(4,128)(2,1)} %x_hbm.1, s32[64,384]{1,0:T(8,128)} %bitcast.3, s32[384]{0:T(512)} %cnt_hbm.1, f32[1,128]{1,0:T(1,128)} %bitcast.5, ...), custom_call_target="tpu_custom_call" | custom-call | tf_op jit(solution)/shard_map/pallas_call | solution.py:397
  92.3 1.2 %shard_map.103 = (f32[384,128]{1,0:T(8,128)}, bf16[3,2048]{1,0:T(4,128)(2,1)}, bf16[128,2048]{1,0:T(8,128)(2,1)}, bf16[128,2048]{1,0:T(8,128)(2,1)}) custom-call(f32[384,128]{1,0:T(8,128)S(1)} %get-tuple-element.9.pre_ref, bf16[3,2048]{1,0:T(4,128)(2,1)S(1)} %get-tuple-element.10.res_ref, bf16[128,2048]{1,0:T(8,128)(2,1)S(1)} %get-tuple-element.11.gd_ref, ...), custom_call_target="tpu_custom_call" | custom-call | tf_op jit(solution)/shard_map/pallas_call | solution.py:457

commit v4 on v3

--- a/solution.py
+++ b/solution.py
@@ -27,8 +27,6 @@
         self.lat = lat_dev
         self.top = top_count
         self.chunk = self.rows // self.X
-        self.parts = 4
-        self.part_cols = self.width // self.parts
 
 
 def kernel(
@@ -41,7 +39,6 @@
 ):
     n, X, own, block, width, lanes, flat = dm.n, dm.X, dm.own, dm.block, dm.width, dm.lanes, dm.flat
     rows, lat, chunk = dm.rows, dm.lat, dm.chunk
-    parts, part_cols = dm.parts, dm.part_cols
     depth = n // 2
     L = lax.axis_index("lat")
     t = lax.axis_index("tok")
@@ -158,12 +155,6 @@
         m = jnp.where(local_ids[k : k + 1, :] == lat_i, 1.0, m)
     mask_all[...] = m.T
     mask[...] = mask_all[my_rows, :]
-
-    def far_parts(way):
-        return range(parts // 2) if way == 1 else range(parts // 2, parts)
-
-    def near_parts(way):
-        return far_parts(-way)
 
     def block_rows(pos):
         return pl.ds(pl.multiple_of(pos * block, 16), block)
@@ -275,25 +266,28 @@
     def rebuild(pos):
         at = block_rows(pos)
         value = jnp.dot(act_f[at, :], WD[...], preferred_element_type=F32)
-        for h in range(parts):
-            T[h, at, :] = value[:, h * part_cols : (h + 1) * part_cols]
-
+        for j in range(lanes):
+            T[j, at, :] = value[:, j * 128 : (j + 1) * 128]
+
+    by_way = sorted(range(n), key=lambda d: -min(d, n - d))
     flying = {}
 
+    def hops_of(k, way):
+        return depth if (k % 2 == 0) == (way == 1) else depth - 1
+
     def ring_reduce_hop(i):
-        for k in range(parts):
+        for k, d in enumerate(by_way):
             for way in (1, -1):
-                far = k < parts // 2
-                h = (*far_parts(way), *near_parts(way))[k]
-                hops = depth if far else depth - 1
+                hops = hops_of(k, way)
                 if i > hops:
                     continue
+                col = wrap(a + d, n)
                 at = block_rows(wrap(b + way * (hops + 1 - i), n))
                 w = 0 if way == 1 else 1
                 if i > 1:
-                    flying[way, i - 1, h].wait_recv()
-                    T[h, at, :] = T[h, at, :] + RB[w, i - 2, h]
-                flying[way, i, h] = go(remote(T.at[h, at], RB.at[w, i - 1, h], lat_of(a, wrap(b + way, n)), t))
+                    flying[way, i - 1, k].wait_recv()
+                    T[col, at, :] = T[col, at, :] + RB[w, i - 2, k]
+                flying[way, i, k] = go(remote(T.at[col, at], RB.at[w, i - 1, k], lat_of(a, wrap(b + way, n)), t))
 
     rebuild(wrap(b + depth, n))
     for k in range(depth - 1, 0, -1):
@@ -304,21 +298,18 @@
     rebuild(b)
     for i in range(2, depth + 1):
         ring_reduce_hop(i)
-    for h in (*near_parts(1), *far_parts(1)):
-        q = T[h, my_block, :]
+    q_recv = {}
+    for k, d in enumerate(by_way):
+        q = T[wrap(a + d, n), my_block, :]
         for way in (1, -1):
-            hops = depth if h in far_parts(way) else depth - 1
-            flying[way, hops, h].wait_recv()
-            q = q + RB[0 if way == 1 else 1, hops - 1, h]
-        for j in range(part_cols // 128):
-            Q[h * (part_cols // 128) + j] = q[:, j * 128 : (j + 1) * 128]
-    q_recv = []
-    for d in range(1, n):
-        to = wrap(a + d, n)
-        q_recv.append(go(remote(Q.at[to], RQ.at[d - 1], lat_of(to, b), t)))
-    piece = Q[a]
-    for d in range(1, n):
-        q_recv[d - 1].wait_recv()
+            flying[way, hops_of(k, way), k].wait_recv()
+            q = q + RB[0 if way == 1 else 1, hops_of(k, way) - 1, k]
+        Q[d] = q
+        if d:
+            q_recv[d] = go(remote(Q.at[d], RQ.at[d - 1], lat_of(wrap(a + d, n), b), t))
+    piece = Q[0]
+    for d in sorted(q_recv, key=lambda d: min(d, n - d)):
+        q_recv[d].wait_recv()
         piece = piece + RQ[d - 1]
     a_cols = pl.ds(pl.multiple_of(a * 128, 128), 128)
     db_cols = pl.ds(pl.multiple_of(c * width + a * 128, 128), 128)
@@ -426,8 +417,8 @@
             pltpu.VMEM((dm.chunk, lat), BF16),
             pltpu.VMEM((rows, 2 * lat), BF16),
             pltpu.VMEM((dm.chunk, lat), F32),
-            pltpu.VMEM((dm.parts, rows, dm.part_cols), F32),
-            pltpu.VMEM((2, n // 2, dm.parts, block, dm.part_cols), F32),
+            pltpu.VMEM((dm.lanes, rows, 128), F32),
+            pltpu.VMEM((2, n // 2, n, block, 128), F32),
             pltpu.VMEM((n, block, 128), F32),
             pltpu.VMEM((n - 1, block, 128), F32),
             pltpu.VMEM((dm.lanes, rows, 128), BF16),

time: 93.7 us -> 90.8 us (0.969)
  Pallas kernels: 92.9 us -> 90 us
    pallas_call x1, Pallas kernels: 91.7 us -> 88.8 us  [shards(): pl.pallas_call(functools.partial(kernel, dm), out_shape=(jax.ShapeDtypeSt...]
where the time goes in v4:
time: 90.8 us; the launch traced here: 90.6 us
  Pallas kernels  90 us (99%)
    pallas_call x1, Pallas kernels, shards(): pl.pallas_call(functools.partial(kernel, dm), out_shape=(jax.ShapeDtypeSt...  88.8 us

profile of v4, /device:TPU:1, one launch (start us, length us, event | category | flops | bytes accessed | tf_op | source)
XLA Modules:
  0.0 90.6 jit_solution(108391426111459893)
XLA Ops:
  0.6 88.8 %shard_map.102 = (f32[384,128]{1,0:T(8,128)S(1)}, bf16[3,2048]{1,0:T(4,128)(2,1)S(1)}, bf16[128,2048]{1,0:T(8,128)(2,1)S(1)}, bf16[384,128]{1,0:T(8,128)(2,1)S(1)}, bf16[2,384,1024]{2,1,0:T(8,128)(2,1)S(1)}) custom-call(bf16[3,2048]{1,0:T(4,128)(2,1)} %x_hbm.1, s32[64,384]{1,0:T(8,128)} %bitcast.3, s32[384]{0:T(512)} %cnt_hbm.1, f32[1,128]{1,0:T(1,128)} %bitcast.5, ...), custom_call_target="tpu_custom_call" | custom-call | tf_op jit(solution)/shard_map/pallas_call | solution.py:388
  89.4 1.2 %shard_map.103 = (f32[384,128]{1,0:T(8,128)}, bf16[3,2048]{1,0:T(4,128)(2,1)}, bf16[128,2048]{1,0:T(8,128)(2,1)}, bf16[128,2048]{1,0:T(8,128)(2,1)}) custom-call(f32[384,128]{1,0:T(8,128)S(1)} %get-tuple-element.9.pre_ref, bf16[3,2048]{1,0:T(4,128)(2,1)S(1)} %get-tuple-element.10.res_ref, bf16[128,2048]{1,0:T(8,128)(2,1)S(1)} %get-tuple-element.11.gd_ref, ...), custom_call_target="tpu_custom_call" | custom-call | tf_op jit(solution)/shard_map/pallas_call | solution.py:448

commit v5 on v4

--- a/solution.py
+++ b/solution.py
@@ -34,7 +34,7 @@
     x_hbm, ids_hbm, cnt_hbm, eb_hbm, db_hbm, enc_ref, dec_ref,
     pre_f, res_out, gd_out, ag_f, XF,
     xs, ids_ref, cnt_ref, eb_ref, db_ref, F32S, F, X3, XL, WE, WD, PS, PR, SUM, RX, mask_all, mask, act_s, act_f, pre_s,
-    T, RB, Q, RQ, RES, RESF, ag_s,
+    T, RB, RF, Q, RQ, RES, RESF, ag_s,
     send, recv, local,
 ):
     n, X, own, block, width, lanes, flat = dm.n, dm.X, dm.own, dm.block, dm.width, dm.lanes, dm.flat
@@ -272,38 +272,45 @@
     by_way = sorted(range(n), key=lambda d: -min(d, n - d))
     flying = {}
 
-    def hops_of(k, way):
-        return depth if (k % 2 == 0) == (way == 1) else depth - 1
+    def send_far():
+        col_rows = block_rows(wrap(b + depth, n))
+        for k, d in enumerate(by_way):
+            way = 1 if k % 2 == 0 else -1
+            flying[way, 0, k] = go(
+                remote(T.at[wrap(a + d, n), col_rows], RF.at[k], lat_of(a, wrap(b + 2 * way, n)), t)
+            )
 
     def ring_reduce_hop(i):
         for k, d in enumerate(by_way):
+            col = wrap(a + d, n)
             for way in (1, -1):
-                hops = hops_of(k, way)
-                if i > hops:
-                    continue
-                col = wrap(a + d, n)
-                at = block_rows(wrap(b + way * (hops + 1 - i), n))
+                at = block_rows(wrap(b + way * (depth - i), n))
                 w = 0 if way == 1 else 1
                 if i > 1:
                     flying[way, i - 1, k].wait_recv()
-                    T[col, at, :] = T[col, at, :] + RB[w, i - 2, k]
+                    value = T[col, at, :] + RB[w, i - 2, k]
+                    if i == 2 and (way, 0, k) in flying:
+                        flying[way, 0, k].wait_recv()
+                        value = value + RF[k]
+                    T[col, at, :] = value
                 flying[way, i, k] = go(remote(T.at[col, at], RB.at[w, i - 1, k], lat_of(a, wrap(b + way, n)), t))
 
     rebuild(wrap(b + depth, n))
+    send_far()
     for k in range(depth - 1, 0, -1):
         rebuild(wrap(b + k, n))
         rebuild(wrap(b - k, n))
         if k == depth - 1:
             ring_reduce_hop(1)
     rebuild(b)
-    for i in range(2, depth + 1):
+    for i in range(2, depth):
         ring_reduce_hop(i)
     q_recv = {}
     for k, d in enumerate(by_way):
         q = T[wrap(a + d, n), my_block, :]
         for way in (1, -1):
-            flying[way, hops_of(k, way), k].wait_recv()
-            q = q + RB[0 if way == 1 else 1, hops_of(k, way) - 1, k]
+            flying[way, depth - 1, k].wait_recv()
+            q = q + RB[0 if way == 1 else 1, depth - 2, k]
         Q[d] = q
         if d:
             q_recv[d] = go(remote(Q.at[d], RQ.at[d - 1], lat_of(wrap(a + d, n), b), t))
@@ -418,7 +425,8 @@
             pltpu.VMEM((rows, 2 * lat), BF16),
             pltpu.VMEM((dm.chunk, lat), F32),
             pltpu.VMEM((dm.lanes, rows, 128), F32),
-            pltpu.VMEM((2, n // 2, n, block, 128), F32),
+            pltpu.VMEM((2, n // 2 - 1, n, block, 128), F32),
+            pltpu.VMEM((n, block, 128), F32),
             pltpu.VMEM((n, block, 128), F32),
             pltpu.VMEM((n - 1, block, 128), F32),
             pltpu.VMEM((dm.lanes, rows, 128), BF16),

time: 90.8 us -> 90.1 us (level)
  no operation moved by 1% of the time
where the time goes in v5:
time: 90.1 us; the launch traced here: 90 us
  Pallas kernels  89.3 us (99%)
    pallas_call x1, Pallas kernels, shards(): pl.pallas_call(functools.partial(kernel, dm), out_shape=(jax.ShapeDtypeSt...  88.1 us

profile of v5, /device:TPU:1, one launch (start us, length us, event | category | flops | bytes accessed | tf_op | source)
XLA Modules:
  0.0 90.0 jit_solution(14660772690269353706)
XLA Ops:
  0.6 88.1 %shard_map.102 = (f32[384,128]{1,0:T(8,128)S(1)}, bf16[3,2048]{1,0:T(4,128)(2,1)S(1)}, bf16[128,2048]{1,0:T(8,128)(2,1)S(1)}, bf16[384,128]{1,0:T(8,128)(2,1)S(1)}, bf16[2,384,1024]{2,1,0:T(8,128)(2,1)S(1)}) custom-call(bf16[3,2048]{1,0:T(4,128)(2,1)} %x_hbm.1, s32[64,384]{1,0:T(8,128)} %bitcast.3, s32[384]{0:T(512)} %cnt_hbm.1, f32[1,128]{1,0:T(1,128)} %bitcast.5, ...), custom_call_target="tpu_custom_call" | custom-call | tf_op jit(solution)/shard_map/pallas_call | solution.py:395
  88.7 1.2 %shard_map.103 = (f32[384,128]{1,0:T(8,128)}, bf16[3,2048]{1,0:T(4,128)(2,1)}, bf16[128,2048]{1,0:T(8,128)(2,1)}, bf16[128,2048]{1,0:T(8,128)(2,1)}) custom-call(f32[384,128]{1,0:T(8,128)S(1)} %get-tuple-element.9.pre_ref, bf16[3,2048]{1,0:T(4,128)(2,1)S(1)} %get-tuple-element.10.res_ref, bf16[128,2048]{1,0:T(8,128)(2,1)S(1)} %get-tuple-element.11.gd_ref, ...), custom_call_target="tpu_custom_call" | custom-call | tf_op jit(solution)/shard_map/pallas_call | solution.py:456
